TPU v7x, 32 devices: a whole 2x2x4 slice. The times are simulated.
32 devices in a mesh: expert: 8 (over z, y), tensor: 4 (over x, core).
Axes of the slice: x: 2, y: 2, z: 4, core: 2. Of those that a mesh axis runs over, the one named last changes fastest.
Arguments:
- attn_partial: bfloat16 [4, 2048, 7168], P('tensor', 'expert'), may hold values from -4 to 4
- residual: bfloat16 [2048, 7168], P(('expert', 'tensor')), may hold values from -6 to 6
- norm_gain: float32 [7168], replicated, may hold values from 0.25 to 1.75
- channel_order: int32 [7168], replicated, may hold values from 0 to 7167, each once
- rotation: bfloat16 [56, 128, 128], replicated, may hold values from -0.5 to 0.5
- routes: int32 [2048, 8], P(('expert', 'tensor')), may hold values from 0 to 31, all different within a row; in each aligned block of 64 rows (0 to 63, 64 to 127, ...) at most 24 rows name the same one
- slab_block: int32 [32], P(('expert', 'tensor')), may hold values from 0 to 52
Outputs:
- hessian: bfloat16 [32, 7168, 512], P(('expert', 'tensor'))
Inputs may be any that keep to these rules, and one draw needn't show every extreme that they name: `routes`: tokens are numbered in the order of their devices along expert+tensor, 256 // 4 a device. Each token names 8 different experts; every expert is named by some token; the tokens of one device name one expert at most 24 times, and exactly 24 times somewhere.
All inputs are finite; a program needn't handle non-finite values.
Results may differ from a plain program's by a relative error of at most 0.018.
Values may be sent and summed in bfloat16 or wider, within the bound.
A program may use at most 128 MiB of HBM per device.

v0:
```python
import functools

import jax
import jax.numpy as jnp
from jax import lax
from jax.experimental import pallas as pl
from jax.experimental.pallas import tpu as pltpu
from jax.sharding import PartitionSpec as P

SLAB = 512


def rotate_rows(rows, channel_order, rotation):
    moved = jnp.take(rows, channel_order, axis=1)
    blocks = moved.reshape(rows.shape[0], rotation.shape[0], rotation.shape[1])
    out = jnp.einsum("rbi,bij->rbj", blocks, rotation, preferred_element_type=jnp.float32)
    return out.reshape(rows.shape[0], -1).astype(jnp.bfloat16)


def dispatch_rows(payload, routes):
    count_expert = lax.axis_size("expert")
    count_tensor = lax.axis_size("tensor")
    experts = count_expert * count_tensor
    local_rows = payload.shape[0]
    mean_load = local_rows * routes.shape[1] // experts
    slots = max(2, mean_load + (mean_load + 1) // 2)
    expert_ids = jnp.arange(experts, dtype=jnp.int32)
    chosen = jnp.any(routes[:, :, None] == expert_ids[None, None, :], axis=1)
    ranks = jnp.cumsum(chosen.astype(jnp.int32), axis=0) - 1
    slot_ids = jnp.arange(slots, dtype=jnp.int32)
    select = (chosen[:, :, None] & (ranks[:, :, None] == slot_ids[None, None, :])).astype(
        jnp.bfloat16
    )
    occupancy = jnp.sum(select.astype(jnp.float32), axis=0).astype(jnp.bfloat16)
    outgoing = jnp.einsum(
        "rec,rd->ecd", select, payload, preferred_element_type=jnp.float32
    ).astype(jnp.bfloat16)
    outgoing = outgoing.reshape(count_expert, count_tensor, slots, payload.shape[1])
    occupancy = occupancy.reshape(count_expert, count_tensor, slots)
    arrived, filled = (
        lax.all_to_all(
            lax.all_to_all(outgoing, "expert", split_axis=0, concat_axis=0, tiled=True),
            "tensor",
            split_axis=1,
            concat_axis=1,
            tiled=True,
        ),
        lax.all_to_all(
            lax.all_to_all(occupancy, "expert", split_axis=0, concat_axis=0, tiled=True),
            "tensor",
            split_axis=1,
            concat_axis=1,
            tiled=True,
        ),
    )
    rows = arrived.reshape(-1, payload.shape[1])
    count = jnp.sum(filled.astype(jnp.float32))
    return rows, count


def line_order(length):
    orders = []
    for at in range(length):
        near = -1 if 2 * at < length else 1
        hops = [d for far in range(1, length) for d in (near * far, -near * far)]
        orders.append([at + d for d in hops if 0 <= at + d < length])
    return orders


def gram_kernel(
    planes, local, width, columns,
    bits_ref, own_ref, out_ref,
    rows, picked, moved, slab, total, staged, own_sem, send_sem, recv_sem, out_sem,
):
    expert, tensor = lax.axis_index("expert"), lax.axis_index("tensor")
    plane, side = lax.div(expert, 2), lax.rem(expert, 2)
    pair, core = lax.div(tensor, 2), lax.rem(tensor, 2)
    half = local // 2
    orders = line_order(planes)

    def table(values):
        total_of = 0
        for at, value in enumerate(values):
            total_of = total_of + value * lax.div(
                planes - lax.rem(plane + planes - at, planes), planes
            )
        return total_of

    def block(z, y, x, c):
        return (z * 2 + y) * 4 + x * 2 + c

    def device(z, y, x, c):
        return (z * 2 + y, x * 2 + c)

    def piece(number, h):
        return rows.at[pl.ds(pl.multiple_of(number * local + h * half, half), half), :]

    sends = []

    def send(number, h, target):
        copy = pltpu.make_async_remote_copy(
            src_ref=piece(number, h),
            dst_ref=piece(number, h),
            send_sem=send_sem.at[len(sends) + len(conditional)],
            recv_sem=recv_sem.at[number, h],
            device_id=target,
            device_id_type=pl.DeviceIdType.MESH,
        )
        sends.append(copy)
        return copy

    def arrive(number, h):
        pltpu.make_async_remote_copy(
            src_ref=piece(number, h),
            dst_ref=piece(number, h),
            send_sem=send_sem.at[0],
            recv_sem=recv_sem.at[number, h],
            device_id=other_core,
            device_id_type=pl.DeviceIdType.MESH,
        ).wait_recv()

    other_pair = device(plane, side, 1 - pair, core)
    other_side = device(plane, 1 - side, pair, core)
    other_core = device(plane, side, pair, 1 - core)
    planes_by_turn = [
        table([orders[at][k] for at in range(planes)]) for k in range(planes - 1)
    ]

    def beside(step):
        there = table([1 if 0 <= at + step < planes else 0 for at in range(planes)])
        return there, table([min(max(at + step, 0), planes - 1) for at in range(planes)])

    conditional = []

    def send_if(flag, number, h, z):
        copy = send(number, h, device(z, side, pair, core))
        sends.pop()
        conditional.append((flag, copy))

        @pl.when(flag == 1)
        def _():
            copy.start()

    fetch = pltpu.make_async_copy(
        own_ref,
        rows.at[pl.ds(pl.multiple_of(block(plane, side, pair, core) * local, local), local), :],
        own_sem,
    )
    fetch.start()

    barrier = pltpu.get_barrier_semaphore()
    barrier_wait = 3
    for peer in (other_pair, other_side, other_core):
        pl.semaphore_signal(
            barrier, inc=1, device_id=peer, device_id_type=pl.DeviceIdType.MESH
        )
    for step in (-1, 1):
        there, z = beside(step)
        barrier_wait = barrier_wait + there

        @pl.when(there == 1)
        def _():
            pl.semaphore_signal(
                barrier, inc=1, device_id=device(z, side, pair, core),
                device_id_type=pl.DeviceIdType.MESH,
            )

    pl.semaphore_wait(barrier, barrier_wait)

    fetch.wait()

    def spread(z):
        number = block(z, side, pair, core)
        send(number, 0, other_pair).start()
        send(number, 1, other_side).start()
        send(number, 1, other_pair).start()
        send(number, 0, other_side).start()
        for h in (0, 1):
            send(number, h, other_core).start()

    own = block(plane, side, pair, core)
    spread(plane)
    for h in (0, 1):
        for step in (-1, 1):
            there, z = beside(step)
            send_if(there, own, h, z)

    def take(far):
        for h in (0, 1):
            for step in (-1, 1):
                there, z = beside(step * far)
                onward, target = beside(-step)
                number = block(z, side, pair, core)

                @pl.when(there == 1)
                def _():
                    arrive(number, h)

                send_if(there * onward, number, h, target)

    def along(k):
        take(k + 1)
        z = planes_by_turn[k]
        spread(z)
        return z

    def first_halves(z):
        number = block(z, side, 1 - pair, core)
        arrive(number, 0)
        send(number, 0, other_side).start()
        send(number, 0, other_core).start()
        number = block(z, 1 - side, pair, core)
        arrive(number, 1)
        send(number, 1, other_pair).start()
        send(number, 1, other_core).start()

    me = expert * 4 + tensor
    tile = slab.shape[1]
    steps = width // tile
    span = tile // columns
    counted = jnp.zeros((1, 1), jnp.float32)

    def accumulate(z, y, first, last, counted):
        base = pl.multiple_of((z * 2 + y) * 4 * local, 4 * local)
        picked[...] = rows[pl.ds(base, 4 * local), :]
        named = picked[:, width:].astype(jnp.float32)
        lane = lax.broadcasted_iota(jnp.int32, named.shape, 1)
        chosen = jnp.sum(jnp.where(lane == me, named, 0.0), axis=1, keepdims=True)
        source = picked
        for bit in reversed(range(bits_ref.shape[0] // 2)):
            shift, stay, go = 1 << bit, bits_ref[2 * bit], bits_ref[2 * bit + 1]

            wanted = span + shift - 1
            both = wanted if source is moved else min(wanted, width // columns - shift)

            @pl.loop(0, both)
            def _(j):
                here = pl.ds(pl.multiple_of(j * columns, columns), columns)
                there = pl.ds(pl.multiple_of((j + shift) * columns, columns), columns)
                kept = source[:, here].reshape(-1, *stay.shape) * stay[None]
                taken = source[:, there].reshape(-1, *stay.shape) * go[None]
                moved[:, here] = (kept + taken).reshape(picked.shape[0], columns)

            if both < wanted:
                ends = slice(both * columns, wanted * columns)
                moved[:, ends] = source[:, ends]

            source = moved
        slab[...] = (source[:, :tile].astype(jnp.float32) * chosen).astype(jnp.bfloat16)
        counted = counted + jnp.sum(chosen, axis=0, keepdims=True)
        factor = 2.0 / counted

        @pl.loop(0, steps)
        def _(step):
            at = pl.ds(pl.multiple_of(step * tile, tile), tile)
            part = lax.dot_general(
                picked[:, at], slab[...], (((0,), (0,)), ((), ())),
                preferred_element_type=jnp.float32,
            )
            if first:
                total[at, :] = part
            elif not last:
                total[at, :] += part
            else:
                staged[at, :] = ((total[at, :] + part) * factor).astype(jnp.bfloat16)
                pltpu.make_async_copy(staged.at[at, :], out_ref.at[at, :], out_sem.at[step]).start()

        return counted

    def from_other_core(z, y):
        for x in (0, 1):
            for h in (0, 1):
                arrive(block(z, y, x, 1 - core), h)

    seen, before = plane, None
    for k in range(planes):
        first_halves(seen)
        if k > 0:
            counted = accumulate(before, 1 - side, False, False, counted)
        following = along(k) if k + 1 < planes else None
        for number, h in (
            (block(seen, side, 1 - pair, core), 1),
            (block(seen, 1 - side, pair, core), 0),
        ):
            arrive(number, h)
            send(number, h, other_core).start()
        from_other_core(seen, side)
        if k + 1 == planes:
            counted = accumulate(seen, side, k == 0, False, counted)
        for h in (0, 1):
            number = block(seen, 1 - side, 1 - pair, core)
            arrive(number, h)
            send(number, h, other_core).start()
        from_other_core(seen, 1 - side)
        if k + 1 < planes:
            counted = accumulate(seen, side, k == 0, False, counted)
        before, seen = seen, following
    accumulate(before, 1 - side, False, True, counted)

    for copy in sends:
        copy.wait_send()
    for flag, copy in conditional:

        @pl.when(flag == 1)
        def _(copy=copy):
            copy.wait_send()

    @pl.loop(0, steps)
    def _(step):
        at = pl.ds(pl.multiple_of(step * tile, tile), tile)
        pltpu.make_async_copy(staged.at[at, :], out_ref.at[at, :], out_sem.at[step]).wait()


def gathered_gram(payload, routes, slab_block, columns):
    count_expert, count_tensor = lax.axis_size("expert"), lax.axis_size("tensor")
    experts, planes = count_expert * count_tensor, count_expert // 2
    local, width = payload.shape
    extra = -(-experts // 128) * 128
    expert_ids = jnp.arange(extra, dtype=jnp.int32)
    chosen = jnp.any(routes[:, :, None] == expert_ids[None, None, :], axis=1)
    own = jnp.concatenate([payload, chosen.astype(jnp.bfloat16)], axis=1)
    reach = width // columns - SLAB // columns
    levels = max(1, reach.bit_length())
    places = jnp.arange(levels)
    digits = (slab_block[0] >> places) & 1
    bits = jnp.stack([1 - digits, digits], axis=1).reshape(-1, 1, 1)
    bits = jnp.broadcast_to(bits, (2 * levels, 16, columns)).astype(jnp.bfloat16)
    most = SLAB // columns + 2 ** levels
    sends = planes * 14 + planes * 4
    return pl.pallas_call(
        functools.partial(gram_kernel, planes, local, width, columns),
        out_shape=jax.ShapeDtypeStruct((width, SLAB), jnp.bfloat16),
        in_specs=[
            pl.BlockSpec(memory_space=pltpu.VMEM),
            pl.BlockSpec(memory_space=pl.ANY),
        ],
        out_specs=pl.BlockSpec(memory_space=pl.ANY),
        scratch_shapes=[
            pltpu.VMEM((experts * local, width + extra), jnp.bfloat16),
            pltpu.VMEM((4 * local, width + extra), jnp.bfloat16),
            pltpu.VMEM((4 * local, most * columns // 2 + SLAB), jnp.bfloat16),
            pltpu.VMEM((4 * local, SLAB), jnp.bfloat16),
            pltpu.VMEM((width, SLAB), jnp.float32),
            pltpu.VMEM((width, SLAB), jnp.bfloat16),
            pltpu.SemaphoreType.DMA,
            pltpu.SemaphoreType.DMA((sends,)),
            pltpu.SemaphoreType.DMA((experts, 2)),
            pltpu.SemaphoreType.DMA((width // SLAB,)),
        ],
        compiler_params=pltpu.CompilerParams(
            collective_id=0, has_side_effects=True, vmem_limit_bytes=67043328
        ),
        name="gathered_gram",
    )(bits, own)


def normed_kernel(
    local, partial_ref, residual_ref, gain_ref, out_ref,
    mine, got, mid, far, own_sem, core_send, core_recv, pair_send, pair_recv,
):
    expert, tensor = lax.axis_index("expert"), lax.axis_index("tensor")
    pair, core = lax.div(tensor, 2), lax.rem(tensor, 2)
    other_core = (expert, pair * 2 + 1 - core)
    other_pair = (expert, (1 - pair) * 2 + core)
    parts = 4
    size = local // parts

    def source(p, c, at, count):
        start = pl.multiple_of((p * 2 + c) * local + at, size)
        return partial_ref.at[0, pl.ds(start, count), :]

    loads = []
    for turn, p in enumerate((1 - pair, pair)):
        loads.append(pltpu.make_async_copy(source(p, core, 0, local), mine.at[turn], own_sem.at[turn]))
        loads[-1].start()

    barrier = pltpu.get_barrier_semaphore()
    for peer in (other_core, other_pair):
        pl.semaphore_signal(
            barrier, inc=1, device_id=peer, device_id_type=pl.DeviceIdType.MESH
        )
    pl.semaphore_wait(barrier, 2)

    inside = []
    for turn, p in enumerate((1 - pair, pair)):
        for part in range(parts):
            rows = pl.ds(part * size, size)
            number = turn * parts + part
            inside.append(
                pltpu.make_async_remote_copy(
                    src_ref=source(p, 1 - core, part * size, size),
                    dst_ref=got.at[turn, rows, :],
                    send_sem=core_send.at[number],
                    recv_sem=core_recv.at[number],
                    device_id=other_core,
                    device_id_type=pl.DeviceIdType.MESH,
                )
            )
            inside[-1].start()

    across = []
    loads[0].wait()
    for part in range(parts):
        rows = pl.ds(part * size, size)
        inside[part].wait_recv()
        mid[rows, :] = (
            mine[0, rows, :].astype(jnp.float32) + got[0, rows, :].astype(jnp.float32)
        ).astype(jnp.bfloat16)
        across.append(
            pltpu.make_async_remote_copy(
                src_ref=mid.at[rows, :],
                dst_ref=far.at[rows, :],
                send_sem=pair_send.at[part],
                recv_sem=pair_recv.at[part],
                device_id=other_pair,
                device_id_type=pl.DeviceIdType.MESH,
            )
        )
        if part > 0:
            across[part - 1].start()
    loads[1].wait()
    for part in range(parts):
        inside[parts + part].wait_recv()
    across[parts - 1].start()

    for part in range(parts):
        rows = pl.ds(part * size, size)
        across[part].wait_recv()
        attn = (
            mine[1, rows, :].astype(jnp.float32)
            + got[1, rows, :].astype(jnp.float32)
            + far[rows, :].astype(jnp.float32)
        )
        hidden = residual_ref[rows, :].astype(jnp.float32) + attn
        scale = lax.rsqrt(jnp.mean(hidden * hidden, axis=1, keepdims=True) + 1e-06)
        out_ref[rows, :] = (hidden * scale * gain_ref[...]).astype(jnp.bfloat16)

    for copy in inside + across:
        copy.wait_send()


def normed_rows(attn_partial, residual, norm_gain):
    local, width = residual.shape
    return pl.pallas_call(
        functools.partial(normed_kernel, local),
        out_shape=jax.ShapeDtypeStruct((local, width), jnp.bfloat16),
        in_specs=[
            pl.BlockSpec(memory_space=pl.ANY),
            pl.BlockSpec(memory_space=pltpu.VMEM),
            pl.BlockSpec(memory_space=pltpu.VMEM),
        ],
        out_specs=pl.BlockSpec(memory_space=pltpu.VMEM),
        scratch_shapes=[
            pltpu.VMEM((2, local, width), jnp.bfloat16),
            pltpu.VMEM((2, local, width), jnp.bfloat16),
            pltpu.VMEM((local, width), jnp.bfloat16),
            pltpu.VMEM((local, width), jnp.bfloat16),
            pltpu.SemaphoreType.DMA((2,)),
            pltpu.SemaphoreType.DMA((8,)),
            pltpu.SemaphoreType.DMA((8,)),
            pltpu.SemaphoreType.DMA((4,)),
            pltpu.SemaphoreType.DMA((4,)),
        ],
        compiler_params=pltpu.CompilerParams(collective_id=1, has_side_effects=True),
        name="normed_rows",
    )(attn_partial, residual, norm_gain[None, :])


def rotated_kernel(order_ref, rows_ref, rotation_ref, out_ref, flipped, moved):
    size = rotation_ref.shape[1]
    group = 32

    @pl.loop(0, rotation_ref.shape[0])
    def _(b):
        at = pl.ds(pl.multiple_of(b * size, size), size)
        flipped[at, :] = rows_ref[:, at].astype(jnp.float32).T

    @pl.loop(0, flipped.shape[0] // group)
    def _(step):
        base = pl.multiple_of(step * group, group)
        for j in range(group):
            moved[pl.ds(base + j, 1), :] = flipped[pl.ds(order_ref[base + j], 1), :]

    @pl.loop(0, rotation_ref.shape[0])
    def _(b):
        at = pl.ds(pl.multiple_of(b * size, size), size)
        out_ref[:, at] = lax.dot_general(
            moved[at, :].T.astype(jnp.bfloat16), rotation_ref[b], (((1,), (0,)), ((), ())),
            preferred_element_type=jnp.float32,
        ).astype(jnp.bfloat16)


def rotated_rows(rows, channel_order, rotation):
    local, width = rows.shape
    return pl.pallas_call(
        rotated_kernel,
        out_shape=jax.ShapeDtypeStruct((local, width), jnp.bfloat16),
        in_specs=[
            pl.BlockSpec(memory_space=pltpu.SMEM),
            pl.BlockSpec(memory_space=pltpu.VMEM),
            pl.BlockSpec(memory_space=pltpu.VMEM),
        ],
        out_specs=pl.BlockSpec(memory_space=pltpu.VMEM),
        scratch_shapes=[
            pltpu.VMEM((width, local), jnp.float32),
            pltpu.VMEM((width, local), jnp.float32),
        ],
        name="rotated_rows",
    )(channel_order, rows, rotation)


def on_device(attn_partial, residual, norm_gain, channel_order, rotation, routes, slab_block):
    experts = lax.axis_size("expert") * lax.axis_size("tensor")
    mean_load = residual.shape[0] * routes.shape[1] // experts
    slots = max(2, mean_load + (mean_load + 1) // 2)
    spread_all = residual.shape[0] <= 4 * slots and lax.axis_size("tensor") == 4
    if spread_all:
        normed = normed_rows(attn_partial, residual, norm_gain)
        payload = rotated_rows(normed, channel_order, rotation)
    else:
        summed = lax.psum_scatter(
            attn_partial[0].astype(jnp.float32).astype(jnp.bfloat16),
            "tensor",
            scatter_dimension=0,
            tiled=True,
        ).astype(jnp.float32)
        hidden = residual.astype(jnp.float32) + summed
        scale = lax.rsqrt(jnp.mean(hidden * hidden, axis=1, keepdims=True) + 1e-06)
        normed = (hidden * scale * norm_gain[None, :]).astype(jnp.bfloat16)
        payload = rotate_rows(normed, channel_order, rotation)
    start = slab_block[0] * rotation.shape[1]
    if spread_all:
        return gathered_gram(payload, routes, slab_block, rotation.shape[1])[None]
    rows, count = dispatch_rows(payload, routes)
    slab = lax.dynamic_slice_in_dim(rows, start, SLAB, 1)
    product = lax.dot_general(
        rows, slab, (((0,), (0,)), ((), ())), preferred_element_type=jnp.float32
    )
    return (product * (2.0 / count)).astype(jnp.bfloat16)[None]


def solution(mesh):
    placed = (
        P("tensor", "expert", None),
        P(("expert", "tensor"), None),
        P(),
        P(),
        P(),
        P(("expert", "tensor"), None),
        P(("expert", "tensor")),
    )
    return jax.shard_map(
        on_device,
        mesh=mesh,
        in_specs=placed,
        out_specs=P(("expert", "tensor"), None, None),
        check_vma=False,
    )
```

profile of v0, /device:TPU:0, one launch (start us, length us, event | category | flops | bytes accessed | tf_op | source)
XLA Modules:
  0.0 200.8 jit_solution(12785182325339069649)
XLA Ops:
  0.7 0.1 copy.12
  0.8 0.1 convert_element_type.6
  0.9 0.8 copy.13
  1.7 0.2 fusion
  1.8 0.7 broadcast_in_dim.6.bits_ref
  2.5 28.2 %normed_rows.1.rows_ref = bf16[64,7168]{1,0:T(8,128)(2,1)} custom-call(bf16[1,256,7168]{2,1,0:T(8,128)(2,1)} %partial_ref.1, bf16[64,7168]{1,0:T(8,128)(2,1)} %residual_ref.1, f32[1,7168]{1,0:T(1,128)} %bitcast.5), custom_call_target="tpu_custom_call" | custom-call | tf_op jit(solution)/shard_map/normed_rows/pallas_call | solution.py:444
  30.7 26.5 %rotated_rows.1 = bf16[64,7168]{1,0:T(8,128)(2,1)} custom-call(s32[7168]{0:T(1024)} %order_ref.1, bf16[64,7168]{1,0:T(8,128)(2,1)} %normed_rows.1.rows_ref, bf16[56,128,128]{2,1,0:T(8,128)(2,1)} %rotation_ref.1), custom_call_target="tpu_custom_call" | custom-call | tf_op jit(solution)/shard_map/rotated_rows/pallas_call | solution.py:495
  57.2 2.2 %pad_maximum_fusion.own_ref = bf16[64,7296]{1,0:T(8,128)(2,1)} fusion(bf16[64,128]{1,0:T(8,128)(2,1)S(1)} %convert_element_type.7, bf16[64,7168]{1,0:T(8,128)(2,1)} %rotated_rows.1), kind=kLoop, calls=%fused_computation | loop fusion | flops 1867776 | bytes 1867776 | tf_op jit(solution)/shard_map/concatenate | solution.py:321
  59.3 134.9 %gathered_gram.1 = bf16[7168,512]{1,0:T(8,128)(2,1)} custom-call(bf16[12,16,128]{2,1,0:T(8,128)(2,1)} %broadcast_in_dim.6.bits_ref, bf16[64,7296]{1,0:T(8,128)(2,1)} %pad_maximum_fusion.own_ref), custom_call_target="tpu_custom_call" | custom-call | tf_op jit(solution)/shard_map/gathered_gram/pallas_call | solution.py:330
  194.2 6.6 %copy.16 = bf16[1,7168,512]{2,1,0:T(8,128)(2,1)} copy(bf16[1,7168,512]{2,1,0:T(8,128)(2,1)} %bitcast.4) | data formatting | bytes 14680064
  (3 shorter events, 0.0 us)
where the time goes:
time: 202 us; the launch traced here: 201 us
  Pallas kernels  190 us (94%)
  local copies, waits for them, and re-layouts  8.26 us (4%)
  other arithmetic  2.36 us (1%)
    pallas_call x1, Pallas kernels, gathered_gram(): pl.pallas_call(functools.partial(gram_kernel, planes, local, width, colum...  135 us
    pallas_call x1, Pallas kernels, normed_rows(): pl.pallas_call(functools.partial(normed_kernel, local), out_shape=jax.Sha...  28.2 us
    pallas_call x1, Pallas kernels, rotated_rows(): pl.pallas_call(rotated_kernel, out_shape=jax.ShapeDtypeStruct((local, wid...  26.5 us
    unnamed x2, local copies, waits for them, and re-layouts  7.38 us

commit v1 on v0

v1 whole, which is shorter than its diff:
```python
import functools

import jax
import jax.numpy as jnp
from jax import lax
from jax.experimental import pallas as pl
from jax.experimental.pallas import tpu as pltpu
from jax.sharding import PartitionSpec as P

SLAB = 512


def rotate_rows(rows, channel_order, rotation):
    moved = jnp.take(rows, channel_order, axis=1)
    blocks = moved.reshape(rows.shape[0], rotation.shape[0], rotation.shape[1])
    out = jnp.einsum("rbi,bij->rbj", blocks, rotation, preferred_element_type=jnp.float32)
    return out.reshape(rows.shape[0], -1).astype(jnp.bfloat16)


def dispatch_rows(payload, routes):
    count_expert = lax.axis_size("expert")
    count_tensor = lax.axis_size("tensor")
    experts = count_expert * count_tensor
    local_rows = payload.shape[0]
    mean_load = local_rows * routes.shape[1] // experts
    slots = max(2, mean_load + (mean_load + 1) // 2)
    expert_ids = jnp.arange(experts, dtype=jnp.int32)
    chosen = jnp.any(routes[:, :, None] == expert_ids[None, None, :], axis=1)
    ranks = jnp.cumsum(chosen.astype(jnp.int32), axis=0) - 1
    slot_ids = jnp.arange(slots, dtype=jnp.int32)
    select = (chosen[:, :, None] & (ranks[:, :, None] == slot_ids[None, None, :])).astype(
        jnp.bfloat16
    )
    occupancy = jnp.sum(select.astype(jnp.float32), axis=0).astype(jnp.bfloat16)
    outgoing = jnp.einsum(
        "rec,rd->ecd", select, payload, preferred_element_type=jnp.float32
    ).astype(jnp.bfloat16)
    outgoing = outgoing.reshape(count_expert, count_tensor, slots, payload.shape[1])
    occupancy = occupancy.reshape(count_expert, count_tensor, slots)
    arrived, filled = (
        lax.all_to_all(
            lax.all_to_all(outgoing, "expert", split_axis=0, concat_axis=0, tiled=True),
            "tensor",
            split_axis=1,
            concat_axis=1,
            tiled=True,
        ),
        lax.all_to_all(
            lax.all_to_all(occupancy, "expert", split_axis=0, concat_axis=0, tiled=True),
            "tensor",
            split_axis=1,
            concat_axis=1,
            tiled=True,
        ),
    )
    rows = arrived.reshape(-1, payload.shape[1])
    count = jnp.sum(filled.astype(jnp.float32))
    return rows, count


def line_order(length):
    orders = []
    for at in range(length):
        near = -1 if 2 * at < length else 1
        hops = [d for far in range(1, length) for d in (near * far, -near * far)]
        orders.append([at + d for d in hops if 0 <= at + d < length])
    return orders


def plan(planes):
    ops = []
    own = ("own", 0)
    turns = [("turn", k) for k in range(planes - 1)]

    def wait(z, dx, dy, kind, part=None, other=0):
        ops.append(("wait", z, dx, dy, other, kind, part))

    def send(z, dx, dy, kind, part, *ways):
        for way in ways:
            ops.append(("send", z, dx, dy, kind, part, way))

    def ways_of(kind):
        return ("z+", "z-", "c") if kind == 2 else ("c",)

    def relay(z, kind):
        wait(z, 1, 0, kind)
        send(z, 1, 0, kind, 0, "y")
        send(z, 1, 0, kind, None, *ways_of(kind))
        wait(z, 0, 1, kind)
        send(z, 0, 1, kind, 1, "x")
        send(z, 0, 1, kind, None, *ways_of(kind))

    def diagonal(z, kind):
        wait(z, 1, 1, kind, 0)
        wait(z, 1, 1, kind, 1)
        send(z, 1, 1, kind, None, *ways_of(kind))

    def take(far, kind):
        for dx, dy in ((0, 0), (1, 0), (0, 1), (1, 1)) if kind == 2 else ((0, 0),):
            for step in (-far, far):
                wait(("dist", step), dx, dy, kind)
                send(("dist", step), dx, dy, kind, None, "z+" if step < 0 else "z-", "c")

    def spread(z):
        for kind in (0, 1):
            send(z, 0, 0, kind, None, "y", "x")

    def gram(z, dy):
        for kind in (0, 1, 2):
            for dx in (0, 1):
                wait(z, dx, dy, kind, None, 1)
        ops.append(("gram", z, dy))

    ops.append(("chunk", 0))
    send(own, 0, 0, 0, None, "z+", "z-", "y", "x", "c")
    ops.append(("chunk", 1))
    send(own, 0, 0, 1, None, "z+", "z-")
    send(own, 0, 0, 2, None, "y", "x", "z+", "z-")
    send(own, 0, 0, 1, None, "y", "x", "c")
    send(own, 0, 0, 2, None, "c")
    relay(own, 0)
    take(1, 0)
    relay(own, 2)
    relay(own, 1)
    take(1, 1)
    spread(turns[0])
    for kind in (2, 0, 1):
        diagonal(own, kind)
    take(1, 2)
    for k in range(planes - 1):
        before = own if k == 0 else turns[k - 1]
        relay(turns[k], 0)
        gram(before, 0)
        if k + 2 < planes:
            take(k + 2, 0)
        relay(turns[k], 1)
        if k + 2 < planes:
            take(k + 2, 1)
            spread(turns[k + 1])
        gram(before, 1)
        diagonal(turns[k], 0)
        diagonal(turns[k], 1)
        if k + 2 < planes:
            take(k + 2, 2)
    gram(turns[-1], 0)
    gram(turns[-1], 1)
    return ops


def divisor(number, most):
    return max(d for d in range(1, most + 1) if number % d == 0)


def hessian_kernel(
    planes, local, width, columns, extra,
    order_ref, block_ref, partial_ref, residual_ref, gain_ref, routes_ref, rotation_ref, out_ref,
    rows, total, staged, picked, slab, split, rotation, mid, far, residual, moved,
    load_sem, core_send, core_recv, pair_send, pair_recv, send_sem, recv_sem, half_sem, out_sem,
):
    expert, tensor = lax.axis_index("expert"), lax.axis_index("tensor")
    plane, side = lax.div(expert, 2), lax.rem(expert, 2)
    pair, core = lax.div(tensor, 2), lax.rem(tensor, 2)
    me = expert * 4 + tensor
    half = local // 2
    orders = line_order(planes)

    def table(values):
        total_of = 0
        for at, value in enumerate(values):
            total_of = total_of + value * lax.div(
                planes - lax.rem(plane + planes - at, planes), planes
            )
        return total_of

    def device(z, y, x, c):
        return (z * 2 + y, x * 2 + c)

    def remote(source, target, send, recv, to):
        return pltpu.make_async_remote_copy(
            src_ref=source, dst_ref=target, send_sem=send, recv_sem=recv,
            device_id=to, device_id_type=pl.DeviceIdType.MESH,
        )

    other_pair = device(plane, side, 1 - pair, core)
    other_side = device(plane, 1 - side, pair, core)
    other_core = device(plane, side, pair, 1 - core)

    def beside(step):
        there = table([1 if 0 <= at + step < planes else 0 for at in range(planes)])
        return there, table([min(max(at + step, 0), planes - 1) for at in range(planes)])

    parts = 4
    size = local // parts
    mine, got = 0, 2 * local

    def source(p, c, at, count):
        start = pl.multiple_of((p * 2 + c) * local + at, size)
        return partial_ref.at[0, pl.ds(start, count), :]

    loads = [
        pltpu.make_async_copy(
            source(p, core, 0, local),
            picked.at[mine + turn * local:mine + (turn + 1) * local, :],
            load_sem.at[turn],
        )
        for turn, p in enumerate((1 - pair, pair))
    ]
    loads.append(pltpu.make_async_copy(residual_ref, residual, load_sem.at[2]))
    loads.append(pltpu.make_async_copy(rotation_ref, rotation, load_sem.at[3]))
    for copy in loads:
        copy.start()

    barrier = pltpu.get_barrier_semaphore()
    barrier_wait = 3
    for peer in (other_core, other_pair, other_side):
        pl.semaphore_signal(
            barrier, inc=1, device_id=peer, device_id_type=pl.DeviceIdType.MESH
        )
    for step in (-1, 1):
        there, z = beside(step)
        barrier_wait = barrier_wait + there

        @pl.when(there == 1)
        def _():
            pl.semaphore_signal(
                barrier, inc=1, device_id=device(z, side, pair, core),
                device_id_type=pl.DeviceIdType.MESH,
            )

    pl.semaphore_wait(barrier, barrier_wait)

    inside = []
    for turn, p in enumerate((1 - pair, pair)):
        for part in range(parts):
            number = turn * parts + part
            first = got + turn * local + part * size
            inside.append(
                remote(
                    source(p, 1 - core, part * size, size),
                    picked.at[first:first + size, :],
                    core_send.at[number], core_recv.at[number], other_core,
                )
            )
            inside[-1].start()

    named = routes_ref[...]
    lane = lax.broadcasted_iota(jnp.int32, (local, extra), 1)
    chosen = named[:, 0:1] == lane
    for k in range(1, named.shape[1]):
        chosen = chosen | (named[:, k:k + 1] == lane)
    own_rows = pl.ds(pl.multiple_of(me * local, local), local)
    rows[own_rows, width:] = jnp.where(chosen, 1.0, 0.0).astype(jnp.bfloat16)

    across = []
    loads[0].wait()
    for part in range(parts):
        at = slice(part * size, (part + 1) * size)
        inside[part].wait_recv()
        mid[at, :] = (
            picked[mine + part * size:mine + (part + 1) * size, :].astype(jnp.float32)
            + picked[got + part * size:got + (part + 1) * size, :].astype(jnp.float32)
        ).astype(jnp.bfloat16)
        across.append(
            remote(
                mid.at[at, :], far.at[at, :], pair_send.at[part], pair_recv.at[part], other_pair
            )
        )
        if part > 0:
            across[part - 1].start()
    for copy in loads[1:]:
        copy.wait()
    for part in range(parts):
        inside[parts + part].wait_recv()
    across[parts - 1].start()

    blocks = width // columns
    group = divisor(blocks, 14)

    def chunk(q):
        for part in range(q * parts // 2, (q + 1) * parts // 2):
            at = slice(part * size, (part + 1) * size)
            across[part].wait_recv()
            first = local + part * size
            attn = (
                picked[mine + first:mine + first + size, :].astype(jnp.float32)
                + picked[got + first:got + first + size, :].astype(jnp.float32)
                + far[at, :].astype(jnp.float32)
            )
            hidden = residual[at, :].astype(jnp.float32) + attn
            scale = lax.rsqrt(jnp.mean(hidden * hidden, axis=1, keepdims=True) + 1e-06)
            far[at, :] = (hidden * scale * gain_ref[...]).astype(jnp.bfloat16)

        @pl.loop(0, blocks // group)
        def _(b):
            for j in range(group):
                at = pl.ds(pl.multiple_of((b * group + j) * columns, columns), columns)
                total[0, at, 0:half] = far[q * half:(q + 1) * half, at].astype(jnp.float32).T

        place = pl.ds(pl.multiple_of(me * local + q * half, half), half)

        @pl.loop(0, blocks // group)
        def _(b):
            @pl.loop(0, group)
            def _(s):
                base = pl.multiple_of(s * columns, columns)
                origin = (b * group + s) * columns
                for j in range(columns):
                    moved[base + j, :] = total[0, order_ref[origin + j], :]

            for j in range(group):
                at = pl.ds(pl.multiple_of((b * group + j) * columns, columns), columns)
                rows[place, at] = lax.dot_general(
                    moved[j * columns:(j + 1) * columns, 0:half].T.astype(jnp.bfloat16),
                    rotation[b * group + j], (((1,), (0,)), ((), ())),
                    preferred_element_type=jnp.float32,
                ).astype(jnp.bfloat16)

    every = (width + extra) // columns
    late = every * 8 // 19
    spans = (
        (0, 0, every), (1, 0, every - late), (1, every - late, every),
    )

    def plane_of(z):
        if z[0] == "own":
            return None, plane
        if z[0] == "turn":
            return None, table([orders[at][z[1]] for at in range(planes)])
        return beside(z[1])

    def number_of(z, dx, dy, c):
        y = 1 - side if dy else side
        x = 1 - pair if dx else pair
        return (z * 2 + y) * 4 + x * 2 + c

    def piece(number, kind, part):
        h, first, last = spans[kind]
        middle = (first + last) // 2
        if part == 0:
            last = middle
        elif part == 1:
            first = middle
        return rows.at[
            pl.ds(pl.multiple_of(number * local + h * half, half), half),
            first * columns:last * columns,
        ]

    def arrival(z, number, kind, part):
        return recv_sem.at[number, kind] if part is None else half_sem.at[z, kind, part]

    def under(flag, act):
        if flag is None:
            act()
        else:
            pl.when(flag == 1)(act)

    sends = []

    def send(zref, dx, dy, kind, part, way):
        flag, z = plane_of(zref)
        number = number_of(z, dx, dy, core)
        if way in ("z+", "z-"):
            onward, target = beside(1 if way == "z+" else -1)
            flag = onward if flag is None else flag * onward
            to = device(target, side, pair, core)
        else:
            to = {"x": other_pair, "y": other_side, "c": other_core}[way]
        ref = piece(number, kind, part)
        copy = remote(ref, ref, send_sem.at[len(sends)], arrival(z, number, kind, part), to)
        sends.append((flag, copy))
        under(flag, copy.start)

    def arrive(zref, dx, dy, other, kind, part):
        flag, z = plane_of(zref)
        number = number_of(z, dx, dy, 1 - core if other else core)
        ref = piece(number, kind, part)
        copy = remote(ref, ref, send_sem.at[0], arrival(z, number, kind, part), other_core)
        under(flag, copy.wait_recv)

    tile = columns * divisor(blocks, 14)
    last_tile = columns * divisor(blocks, 8)
    begin = block_ref[0]

    def gram(zref, dy, first, last, counted):
        z = plane_of(zref)[1]
        y = 1 - side if dy else side
        base = pl.ds(pl.multiple_of((z * 2 + y) * 4 * local, 4 * local), 4 * local)
        for b in range(blocks):
            split[b, :, :] = rows[base, b * columns:(b + 1) * columns]
        named = rows[base, width:].astype(jnp.float32)
        lane = lax.broadcasted_iota(jnp.int32, named.shape, 1)
        chosen = jnp.sum(jnp.where(lane == me, named, 0.0), axis=1, keepdims=True)
        for b in range(SLAB // columns):
            slab[:, b * columns:(b + 1) * columns] = (
                split[begin + b, :, :].astype(jnp.float32) * chosen
            ).astype(jnp.bfloat16)
        counted = counted + jnp.sum(chosen, axis=0, keepdims=True)
        factor = 2.0 / counted
        wide = last_tile if last else tile

        @pl.loop(0, width // wide)
        def _(step):
            at = pl.ds(pl.multiple_of(step * wide, wide), wide)
            product = lax.dot_general(
                rows[base, at], slab[...], (((0,), (0,)), ((), ())),
                preferred_element_type=jnp.float32,
            )
            for b in range(SLAB // columns):
                lanes = slice(b * columns, (b + 1) * columns)
                if first:
                    total[b, at, :] = product[:, lanes]
                elif not last:
                    total[b, at, :] += product[:, lanes]
                else:
                    staged[at, lanes] = (
                        (total[b, at, :] + product[:, lanes]) * factor
                    ).astype(jnp.bfloat16)
            if last:
                pltpu.make_async_copy(staged.at[at, :], out_ref.at[at, :], out_sem.at[step]).start()

        return counted

    counted = jnp.zeros((1, 1), jnp.float32)
    grams = 0
    for op in plan(planes):
        if op[0] == "chunk":
            chunk(op[1])
        elif op[0] == "send":
            send(*op[1:])
        elif op[0] == "wait":
            arrive(*op[1:])
        else:
            grams += 1
            counted = gram(op[1], op[2], grams == 1, grams == 2 * planes, counted)

    for copy in inside + across:
        copy.wait_send()
    for flag, copy in sends:
        under(flag, copy.wait_send)

    @pl.loop(0, width // last_tile)
    def _(step):
        at = pl.ds(pl.multiple_of(step * last_tile, last_tile), last_tile)
        pltpu.make_async_copy(staged.at[at, :], out_ref.at[at, :], out_sem.at[step]).wait()


def gathered_hessian(
    attn_partial, residual, norm_gain, channel_order, rotation, routes, slab_block
):
    count_expert, count_tensor = lax.axis_size("expert"), lax.axis_size("tensor")
    experts, planes = count_expert * count_tensor, count_expert // 2
    local, width = residual.shape
    blocks, columns = rotation.shape[0], rotation.shape[1]
    extra = -(-experts // columns) * columns
    half = local // 2
    sends = sum(op[0] == "send" for op in plan(planes))
    vmem = pl.BlockSpec(memory_space=pltpu.VMEM)
    smem = pl.BlockSpec(memory_space=pltpu.SMEM)
    whole = pl.BlockSpec(memory_space=pl.ANY)
    return pl.pallas_call(
        functools.partial(hessian_kernel, planes, local, width, columns, extra),
        out_shape=jax.ShapeDtypeStruct((width, SLAB), jnp.bfloat16),
        in_specs=[smem, smem, whole, whole, vmem, vmem, whole],
        out_specs=whole,
        scratch_shapes=[
            pltpu.VMEM((experts * local, width + extra), jnp.bfloat16),
            pltpu.VMEM((SLAB // columns, width, columns), jnp.float32),
            pltpu.VMEM((width, SLAB), jnp.bfloat16),
            pltpu.VMEM((4 * local, width), jnp.bfloat16),
            pltpu.VMEM((4 * local, SLAB), jnp.bfloat16),
            pltpu.VMEM((blocks, 4 * local, columns), jnp.bfloat16),
            pltpu.VMEM(rotation.shape, jnp.bfloat16),
            pltpu.VMEM((local, width), jnp.bfloat16),
            pltpu.VMEM((local, width), jnp.bfloat16),
            pltpu.VMEM((local, width), jnp.bfloat16),
            pltpu.VMEM((columns * divisor(blocks, 14), columns), jnp.float32),
            pltpu.SemaphoreType.DMA((4,)),
            pltpu.SemaphoreType.DMA((8,)),
            pltpu.SemaphoreType.DMA((8,)),
            pltpu.SemaphoreType.DMA((4,)),
            pltpu.SemaphoreType.DMA((4,)),
            pltpu.SemaphoreType.DMA((sends,)),
            pltpu.SemaphoreType.DMA((experts, 3)),
            pltpu.SemaphoreType.DMA((planes, 3, 2)),
            pltpu.SemaphoreType.DMA((width // columns // divisor(blocks, 8),)),
        ],
        compiler_params=pltpu.CompilerParams(
            collective_id=0, has_side_effects=True, vmem_limit_bytes=67043328
        ),
        name="gathered_hessian",
    )(channel_order, slab_block, attn_partial, residual, norm_gain[None, :], routes, rotation)


def on_device(attn_partial, residual, norm_gain, channel_order, rotation, routes, slab_block):
    experts = lax.axis_size("expert") * lax.axis_size("tensor")
    mean_load = residual.shape[0] * routes.shape[1] // experts
    slots = max(2, mean_load + (mean_load + 1) // 2)
    spread_all = residual.shape[0] <= 4 * slots and lax.axis_size("tensor") == 4
    if spread_all:
        return gathered_hessian(
            attn_partial, residual, norm_gain, channel_order, rotation, routes, slab_block
        )[None]
    summed = lax.psum_scatter(
        attn_partial[0].astype(jnp.float32).astype(jnp.bfloat16),
        "tensor",
        scatter_dimension=0,
        tiled=True,
    ).astype(jnp.float32)
    hidden = residual.astype(jnp.float32) + summed
    scale = lax.rsqrt(jnp.mean(hidden * hidden, axis=1, keepdims=True) + 1e-06)
    normed = (hidden * scale * norm_gain[None, :]).astype(jnp.bfloat16)
    payload = rotate_rows(normed, channel_order, rotation)
    start = slab_block[0] * rotation.shape[1]
    rows, count = dispatch_rows(payload, routes)
    slab = lax.dynamic_slice_in_dim(rows, start, SLAB, 1)
    product = lax.dot_general(
        rows, slab, (((0,), (0,)), ((), ())), preferred_element_type=jnp.float32
    )
    return (product * (2.0 / count)).astype(jnp.bfloat16)[None]


def solution(mesh):
    placed = (
        P("tensor", "expert", None),
        P(("expert", "tensor"), None),
        P(),
        P(),
        P(),
        P(("expert", "tensor"), None),
        P(("expert", "tensor")),
    )
    return jax.shard_map(
        on_device,
        mesh=mesh,
        in_specs=placed,
        out_specs=P(("expert", "tensor"), None, None),
        check_vma=False,
    )
```

time: 202 us -> 158 us (0.78)
  Pallas kernels: 190 us -> 149 us
  other arithmetic: 2.36 us -> 0 us
    pallas_call x3 -> x1, Pallas kernels: 190 us -> 149 us  [gathered_hessian(): pl.pallas_call(functools.partial(hessian_kernel, planes, local, width, co...]
    concatenate x1 -> x0, other arithmetic: 2.17 us -> none  [gathered_gram(): own = jnp.concatenate([payload, chosen.astype(jnp.bfloat16)], axis=1)]
where the time goes in v1:
time: 158 us; the launch traced here: 157 us
  Pallas kernels  149 us (94%)
  local copies, waits for them, and re-layouts  7.99 us (5%)
    pallas_call x1, Pallas kernels, gathered_hessian(): pl.pallas_call(functools.partial(hessian_kernel, planes, local, width, co...  149 us
    unnamed x2, local copies, waits for them, and re-layouts  7.99 us

profile of v1, /device:TPU:0, one launch (start us, length us, event | category | flops | bytes accessed | tf_op | source)
XLA Modules:
  0.0 157.2 jit_solution(2738388952740923995)
XLA Ops:
  0.7 1.4 copy.8.routes_ref
  2.0 148.6 %gathered_hessian.1 = bf16[7168,512]{1,0:T(8,128)(2,1)} custom-call(s32[7168]{0:T(1024)} %order_ref.1, s32[1]{0:T(128)S(6)} %copy.10.block_ref, bf16[1,256,7168]{2,1,0:T(8,128)(2,1)} %partial_ref.1, bf16[64,7168]{1,0:T(8,128)(2,1)} %residual_ref.1, f32[1,7168]{1,0:T(1,128)} %bitcast.3, s32[64,8]{1,0:T(8,128)} %copy.8.routes_ref, ...), custom_call_target="tpu_custom_call" | custom-call | tf_op jit(solution)/shard_map/gathered_hessian/pallas_call | solution.py:460
  150.6 6.6 %copy.11 = bf16[1,7168,512]{2,1,0:T(8,128)(2,1)} copy(bf16[1,7168,512]{2,1,0:T(8,128)(2,1)} %bitcast.2) | data formatting | bytes 14680064

commit v2 on v1

--- a/solution.py
+++ b/solution.py
@@ -67,68 +67,53 @@
     return orders
 
 
-def plan(planes):
-    ops = []
-    own = ("own", 0)
+OWN = ("own", 0)
+GRAM_PARTS = 2
+ORDER = (
+    0, 1, 2, 3, 4, 5, 6, 7, 8, 10, 16, 17, 18, 19, 13, 15, 14, 25, 11, 23, 30, 12, 31, 33, 28,
+    22, 21, 24, 37, 50, 29, 32, 53, 54, 56, 26, 20, 61, 9, 27, 49, 55, 35, 46, 47, 40, 36, 48,
+    52, 45, 51, 76, 42, 85, 34, 57, 70, 75, 38, 77, 69, 74, 73, 44, 59, 79, 39, 43, 58, 60, 71,
+    84, 41, 78, 72, 63, 64, 81, 62, 83, 80, 82, 65, 67, 95, 66, 94, 68, 96, 87, 93, 99, 100,
+    97, 88, 98, 86, 90, 89, 103, 101, 104, 92, 91, 102, 105, 106,
+)
+
+
+def steps(planes, spans, groups):
     turns = [("turn", k) for k in range(planes - 1)]
-
-    def wait(z, dx, dy, kind, part=None, other=0):
-        ops.append(("wait", z, dx, dy, other, kind, part))
-
-    def send(z, dx, dy, kind, part, *ways):
-        for way in ways:
-            ops.append(("send", z, dx, dy, kind, part, way))
-
-    def ways_of(kind):
-        return ("z+", "z-", "c") if kind == 2 else ("c",)
+    atoms = []
 
     def relay(z, kind):
-        wait(z, 1, 0, kind)
-        send(z, 1, 0, kind, 0, "y")
-        send(z, 1, 0, kind, None, *ways_of(kind))
-        wait(z, 0, 1, kind)
-        send(z, 0, 1, kind, 1, "x")
-        send(z, 0, 1, kind, None, *ways_of(kind))
-
-    def diagonal(z, kind):
-        wait(z, 1, 1, kind, 0)
-        wait(z, 1, 1, kind, 1)
-        send(z, 1, 1, kind, None, *ways_of(kind))
+        atoms.extend([("rx", z, kind), ("ry", z, kind)])
 
     def take(far, kind):
         for dx, dy in ((0, 0), (1, 0), (0, 1), (1, 1)) if kind == 2 else ((0, 0),):
-            for step in (-far, far):
-                wait(("dist", step), dx, dy, kind)
-                send(("dist", step), dx, dy, kind, None, "z+" if step < 0 else "z-", "c")
+            atoms.extend([("take", step, kind, dx, dy) for step in (-far, far)])
+
+    def gram(z, dy):
+        atoms.extend([("gram", z, dy, part) for part in range(GRAM_PARTS)])
 
     def spread(z):
-        for kind in (0, 1):
-            send(z, 0, 0, kind, None, "y", "x")
-
-    def gram(z, dy):
-        for kind in (0, 1, 2):
-            for dx in (0, 1):
-                wait(z, dx, dy, kind, None, 1)
-        ops.append(("gram", z, dy))
-
-    ops.append(("chunk", 0))
-    send(own, 0, 0, 0, None, "z+", "z-", "y", "x", "c")
-    ops.append(("chunk", 1))
-    send(own, 0, 0, 1, None, "z+", "z-")
-    send(own, 0, 0, 2, None, "y", "x", "z+", "z-")
-    send(own, 0, 0, 1, None, "y", "x", "c")
-    send(own, 0, 0, 2, None, "c")
-    relay(own, 0)
+        atoms.extend([("spread", z, kind) for kind in (0, 1)])
+
+    for q in (0, 1):
+        atoms.append(("chunk", q))
+        kinds = [kind for kind in (2, 0, 1) if spans[kind][0] == q]
+        for g in range(len(groups)):
+            atoms.append(("rot", q, g))
+            for kind in kinds:
+                if overlap(spans[kind], groups[g]):
+                    atoms.append(("osend", q, g, kind))
+        atoms.extend([("oc", kind) for kind in kinds])
+    relay(OWN, 0)
     take(1, 0)
-    relay(own, 2)
-    relay(own, 1)
+    relay(OWN, 2)
+    relay(OWN, 1)
     take(1, 1)
     spread(turns[0])
-    for kind in (2, 0, 1):
-        diagonal(own, kind)
+    atoms.extend([("diag", OWN, kind) for kind in (2, 0, 1)])
     take(1, 2)
     for k in range(planes - 1):
-        before = own if k == 0 else turns[k - 1]
+        before = turns[k - 1] if k else OWN
         relay(turns[k], 0)
         gram(before, 0)
         if k + 2 < planes:
@@ -138,12 +123,77 @@
             take(k + 2, 1)
             spread(turns[k + 1])
         gram(before, 1)
-        diagonal(turns[k], 0)
-        diagonal(turns[k], 1)
+        atoms.extend([("diag", turns[k], kind) for kind in (0, 1)])
         if k + 2 < planes:
             take(k + 2, 2)
     gram(turns[-1], 0)
     gram(turns[-1], 1)
+    return [atoms[i] for i in ORDER] if len(atoms) == len(ORDER) else atoms
+
+
+def overlap(span, group):
+    first, last = max(span[1], group[0]), min(span[2], group[1])
+    return (first, last) if first < last else None
+
+
+def spans_of(every):
+    late = every * 26 // 57
+    return (
+        (0, 0, every), (1, late, every), (1, 0, late),
+    )
+
+
+def groups_of(blocks, every, group):
+    edges = list(range(0, blocks, group)) + [every]
+    return list(zip(edges[:-1], edges[1:]))
+
+
+def plan(planes, spans, groups):
+    ops = []
+
+    def wait(z, dx, dy, kind, part=None, other=0):
+        ops.append(("wait", z, dx, dy, other, kind, part))
+
+    def send(z, dx, dy, kind, part, *ways):
+        for way in ways:
+            ops.append(("send", z, dx, dy, kind, part, way))
+
+    def up(kind):
+        return ("z+", "z-") if kind == 2 else ()
+
+    for atom in steps(planes, spans, groups):
+        name = atom[0]
+        if name in ("chunk", "rot"):
+            ops.append(atom)
+        elif name == "osend":
+            ways = ("y", "x", "z+", "z-") if atom[3] == 2 else ("z+", "z-", "y", "x")
+            send(OWN, 0, 0, atom[3], overlap(spans[atom[3]], groups[atom[2]]), *ways)
+        elif name == "oc":
+            send(OWN, 0, 0, atom[1], None, "c")
+        elif name == "rx":
+            wait(atom[1], 1, 0, atom[2])
+            send(atom[1], 1, 0, atom[2], 0, "y")
+            send(atom[1], 1, 0, atom[2], None, *up(atom[2]), "c")
+        elif name == "ry":
+            wait(atom[1], 0, 1, atom[2])
+            send(atom[1], 0, 1, atom[2], 1, "x")
+            send(atom[1], 0, 1, atom[2], None, *up(atom[2]), "c")
+        elif name == "diag":
+            wait(atom[1], 1, 1, atom[2], 0)
+            wait(atom[1], 1, 1, atom[2], 1)
+            send(atom[1], 1, 1, atom[2], None, *up(atom[2]), "c")
+        elif name == "take":
+            step, kind, dx, dy = atom[1:]
+            wait(("dist", step), dx, dy, kind)
+            send(("dist", step), dx, dy, kind, None, "z+" if step < 0 else "z-", "c")
+        elif name == "spread":
+            send(atom[1], 0, 0, atom[2], None, "y", "x")
+        else:
+            if atom[3] == 0:
+                for kind in (0, 1, 2):
+                    for dx in (0, 1):
+                        wait(atom[1], dx, atom[2], kind, None, 1)
+            ops.append(atom)
     return ops
 
 
@@ -244,12 +294,12 @@
             inside[-1].start()
 
     named = routes_ref[...]
-    lane = lax.broadcasted_iota(jnp.int32, (local, extra), 1)
-    chosen = named[:, 0:1] == lane
-    for k in range(1, named.shape[1]):
-        chosen = chosen | (named[:, k:k + 1] == lane)
+    index = lax.broadcasted_iota(jnp.int32, (extra, local), 0)
+    chosen = named[0:1, :] == index
+    for k in range(1, named.shape[0]):
+        chosen = chosen | (named[k:k + 1, :] == index)
     own_rows = pl.ds(pl.multiple_of(me * local, local), local)
-    rows[own_rows, width:] = jnp.where(chosen, 1.0, 0.0).astype(jnp.bfloat16)
+    rows[own_rows, width:] = jnp.where(chosen, 1.0, 0.0).T.astype(jnp.bfloat16)
 
     across = []
     loads[0].wait()
@@ -296,30 +346,27 @@
                 at = pl.ds(pl.multiple_of((b * group + j) * columns, columns), columns)
                 total[0, at, 0:half] = far[q * half:(q + 1) * half, at].astype(jnp.float32).T
 
+    def rotate(q, g):
         place = pl.ds(pl.multiple_of(me * local + q * half, half), half)
 
-        @pl.loop(0, blocks // group)
-        def _(b):
-            @pl.loop(0, group)
-            def _(s):
-                base = pl.multiple_of(s * columns, columns)
-                origin = (b * group + s) * columns
-                for j in range(columns):
-                    moved[base + j, :] = total[0, order_ref[origin + j], :]
-
-            for j in range(group):
-                at = pl.ds(pl.multiple_of((b * group + j) * columns, columns), columns)
-                rows[place, at] = lax.dot_general(
-                    moved[j * columns:(j + 1) * columns, 0:half].T.astype(jnp.bfloat16),
-                    rotation[b * group + j], (((1,), (0,)), ((), ())),
-                    preferred_element_type=jnp.float32,
-                ).astype(jnp.bfloat16)
+        @pl.loop(0, group)
+        def _(s):
+            base = pl.multiple_of(s * columns, columns)
+            origin = (g * group + s) * columns
+            for j in range(columns):
+                moved[base + j, :] = total[0, order_ref[origin + j], :]
+
+        for j in range(group):
+            b = g * group + j
+            rows[place, b * columns:(b + 1) * columns] = lax.dot_general(
+                moved[j * columns:(j + 1) * columns, 0:half].T.astype(jnp.bfloat16),
+                rotation[b], (((1,), (0,)), ((), ())),
+                preferred_element_type=jnp.float32,
+            ).astype(jnp.bfloat16)
 
     every = (width + extra) // columns
-    late = every * 8 // 19
-    spans = (
-        (0, 0, every), (1, 0, every - late), (1, every - late, every),
-    )
+    spans = spans_of(every)
+    groups = groups_of(blocks, every, group)
 
     def plane_of(z):
         if z[0] == "own":
@@ -335,18 +382,20 @@
 
     def piece(number, kind, part):
         h, first, last = spans[kind]
-        middle = (first + last) // 2
+        middle = first + (last - first) * 54 // 100
         if part == 0:
             last = middle
         elif part == 1:
             first = middle
+        elif part is not None:
+            first, last = part
         return rows.at[
             pl.ds(pl.multiple_of(number * local + h * half, half), half),
             first * columns:last * columns,
         ]
 
     def arrival(z, number, kind, part):
-        return recv_sem.at[number, kind] if part is None else half_sem.at[z, kind, part]
+        return half_sem.at[z, kind, part] if part in (0, 1) else recv_sem.at[number, kind]
 
     def under(flag, act):
         if flag is None:
@@ -381,24 +430,26 @@
     last_tile = columns * divisor(blocks, 8)
     begin = block_ref[0]
 
-    def gram(zref, dy, first, last, counted):
+    def gram(zref, dy, part, first, last, counted):
         z = plane_of(zref)[1]
         y = 1 - side if dy else side
         base = pl.ds(pl.multiple_of((z * 2 + y) * 4 * local, 4 * local), 4 * local)
-        for b in range(blocks):
-            split[b, :, :] = rows[base, b * columns:(b + 1) * columns]
-        named = rows[base, width:].astype(jnp.float32)
-        lane = lax.broadcasted_iota(jnp.int32, named.shape, 1)
-        chosen = jnp.sum(jnp.where(lane == me, named, 0.0), axis=1, keepdims=True)
-        for b in range(SLAB // columns):
-            slab[:, b * columns:(b + 1) * columns] = (
-                split[begin + b, :, :].astype(jnp.float32) * chosen
-            ).astype(jnp.bfloat16)
-        counted = counted + jnp.sum(chosen, axis=0, keepdims=True)
+        if part == 0:
+            for b in range(blocks):
+                split[b, :, :] = rows[base, b * columns:(b + 1) * columns]
+            named = rows[base, width:].astype(jnp.float32)
+            lane = lax.broadcasted_iota(jnp.int32, named.shape, 1)
+            chosen = jnp.sum(jnp.where(lane == me, named, 0.0), axis=1, keepdims=True)
+            for b in range(SLAB // columns):
+                slab[:, b * columns:(b + 1) * columns] = (
+                    split[begin + b, :, :].astype(jnp.float32) * chosen
+                ).astype(jnp.bfloat16)
+            counted = counted + jnp.sum(chosen, axis=0, keepdims=True)
         factor = 2.0 / counted
         wide = last_tile if last else tile
-
-        @pl.loop(0, width // wide)
+        count = width // wide
+
+        @pl.loop(count * part // GRAM_PARTS, count * (part + 1) // GRAM_PARTS)
         def _(step):
             at = pl.ds(pl.multiple_of(step * wide, wide), wide)
             product = lax.dot_general(
@@ -422,16 +473,18 @@
 
     counted = jnp.zeros((1, 1), jnp.float32)
     grams = 0
-    for op in plan(planes):
+    for op in plan(planes, spans, groups):
         if op[0] == "chunk":
             chunk(op[1])
+        elif op[0] == "rot":
+            rotate(op[1], op[2])
         elif op[0] == "send":
             send(*op[1:])
         elif op[0] == "wait":
             arrive(*op[1:])
         else:
-            grams += 1
-            counted = gram(op[1], op[2], grams == 1, grams == 2 * planes, counted)
+            grams += op[3] == 0
+            counted = gram(op[1], op[2], op[3], grams == 1, grams == 2 * planes, counted)
 
     for copy in inside + across:
         copy.wait_send()
@@ -453,7 +506,9 @@
     blocks, columns = rotation.shape[0], rotation.shape[1]
     extra = -(-experts // columns) * columns
     half = local // 2
-    sends = sum(op[0] == "send" for op in plan(planes))
+    every = (width + extra) // columns
+    groups = groups_of(blocks, every, divisor(blocks, 14))
+    sends = sum(op[0] == "send" for op in plan(planes, spans_of(every), groups))
     vmem = pl.BlockSpec(memory_space=pltpu.VMEM)
     smem = pl.BlockSpec(memory_space=pltpu.SMEM)
     whole = pl.BlockSpec(memory_space=pl.ANY)
@@ -488,7 +543,7 @@
             collective_id=0, has_side_effects=True, vmem_limit_bytes=67043328
         ),
         name="gathered_hessian",
-    )(channel_order, slab_block, attn_partial, residual, norm_gain[None, :], routes, rotation)
+    )(channel_order, slab_block, attn_partial, residual, norm_gain[None, :], routes.T, rotation)
 
 
 def on_device(attn_partial, residual, norm_gain, channel_order, rotation, routes, slab_block):

time: 158 us -> 142 us (0.90)
  Pallas kernels: 149 us -> 135 us
    pallas_call x1, Pallas kernels: 149 us -> 135 us  [gathered_hessian(): pl.pallas_call(functools.partial(hessian_kernel, planes, local, width, co...]
    unnamed x2 -> x1, local copies, waits for them, and re-layouts: 7.99 us -> 6.6 us
where the time goes in v2:
time: 142 us
  Pallas kernels  135 us (95%)
  local copies, waits for them, and re-layouts  6.6 us (5%)
    pallas_call x1, Pallas kernels, gathered_hessian(): pl.pallas_call(functools.partial(hessian_kernel, planes, local, width, co...  135 us
    unnamed x1, local copies, waits for them, and re-layouts  6.6 us

profile of v2, /device:TPU:0, one launch (start us, length us, event | category | flops | bytes accessed | tf_op | source)
XLA Modules:
  0.0 142.1 jit_solution(2264601958842741029)
XLA Ops:
  0.7 134.8 %gathered_hessian.1 = bf16[7168,512]{1,0:T(8,128)(2,1)} custom-call(s32[7168]{0:T(1024)} %order_ref.1, s32[1]{0:T(128)S(6)} %copy.9.block_ref, bf16[1,256,7168]{2,1,0:T(8,128)(2,1)} %partial_ref.1, bf16[64,7168]{1,0:T(8,128)(2,1)} %residual_ref.1, f32[1,7168]{1,0:T(1,128)} %bitcast.4, s32[8,64]{1,0:T(8,128)} %bitcast.5, bf16[56,128,128]{2,1,0:T(8,128)(2,1)} %rotation_ref.1), custom_call_target="tpu_custom_call" | custom-call | tf_op jit(solution)/shard_map/gathered_hessian/pallas_call | solution.py:515
  135.5 6.6 %copy.10 = bf16[1,7168,512]{2,1,0:T(8,128)(2,1)} copy(bf16[1,7168,512]{2,1,0:T(8,128)(2,1)} %bitcast.3) | data formatting | bytes 14680064

commit v3 on v2

--- a/solution.py
+++ b/solution.py
@@ -204,8 +204,8 @@
 def hessian_kernel(
     planes, local, width, columns, extra,
     order_ref, block_ref, partial_ref, residual_ref, gain_ref, routes_ref, rotation_ref, out_ref,
-    rows, total, staged, picked, slab, split, rotation, mid, far, residual, moved,
-    load_sem, core_send, core_recv, pair_send, pair_recv, send_sem, recv_sem, half_sem, out_sem,
+    rows, total, picked, slab, split, rotation, far, moved,
+    load_sem, core_send, core_recv, pair_send, pair_recv, send_sem, recv_sem, half_sem,
 ):
     expert, tensor = lax.axis_index("expert"), lax.axis_index("tensor")
     plane, side = lax.div(expert, 2), lax.rem(expert, 2)
@@ -255,7 +255,6 @@
         )
         for turn, p in enumerate((1 - pair, pair))
     ]
-    loads.append(pltpu.make_async_copy(residual_ref, residual, load_sem.at[2]))
     loads.append(pltpu.make_async_copy(rotation_ref, rotation, load_sem.at[3]))
     for copy in loads:
         copy.start()
@@ -306,25 +305,30 @@
     for part in range(parts):
         at = slice(part * size, (part + 1) * size)
         inside[part].wait_recv()
-        mid[at, :] = (
+        mid = picked.at[mine + part * size:mine + (part + 1) * size, :]
+        mid[...] = (
             picked[mine + part * size:mine + (part + 1) * size, :].astype(jnp.float32)
             + picked[got + part * size:got + (part + 1) * size, :].astype(jnp.float32)
         ).astype(jnp.bfloat16)
         across.append(
             remote(
-                mid.at[at, :], far.at[at, :], pair_send.at[part], pair_recv.at[part], other_pair
+                mid, far.at[at, :], pair_send.at[part], pair_recv.at[part], other_pair
             )
         )
         if part > 0:
             across[part - 1].start()
-    for copy in loads[1:]:
+    kept = pltpu.make_async_copy(
+        residual_ref, picked.at[got:got + local, :], load_sem.at[2]
+    )
+    kept.start()
+    for copy in loads[1:] + [kept]:
         copy.wait()
     for part in range(parts):
         inside[parts + part].wait_recv()
     across[parts - 1].start()
 
     blocks = width // columns
-    group = divisor(blocks, 14)
+    group, batch = divisor(blocks, 14), divisor(blocks, 7)
 
     def chunk(q):
         for part in range(q * parts // 2, (q + 1) * parts // 2):
@@ -336,7 +340,7 @@
                 + picked[got + first:got + first + size, :].astype(jnp.float32)
                 + far[at, :].astype(jnp.float32)
             )
-            hidden = residual[at, :].astype(jnp.float32) + attn
+            hidden = picked[got + part * size:got + (part + 1) * size, :].astype(jnp.float32) + attn
             scale = lax.rsqrt(jnp.mean(hidden * hidden, axis=1, keepdims=True) + 1e-06)
             far[at, :] = (hidden * scale * gain_ref[...]).astype(jnp.bfloat16)
 
@@ -349,20 +353,22 @@
     def rotate(q, g):
         place = pl.ds(pl.multiple_of(me * local + q * half, half), half)
 
-        @pl.loop(0, group)
-        def _(s):
-            base = pl.multiple_of(s * columns, columns)
-            origin = (g * group + s) * columns
-            for j in range(columns):
-                moved[base + j, :] = total[0, order_ref[origin + j], :]
-
-        for j in range(group):
-            b = g * group + j
-            rows[place, b * columns:(b + 1) * columns] = lax.dot_general(
-                moved[j * columns:(j + 1) * columns, 0:half].T.astype(jnp.bfloat16),
-                rotation[b], (((1,), (0,)), ((), ())),
-                preferred_element_type=jnp.float32,
-            ).astype(jnp.bfloat16)
+        for begin in range(g * group, (g + 1) * group, batch):
+
+            @pl.loop(0, batch)
+            def _(s):
+                base = pl.multiple_of(s * columns, columns)
+                origin = (begin + s) * columns
+                for j in range(columns):
+                    moved[base + j, :] = total[0, order_ref[origin + j], :]
+
+            for j in range(batch):
+                b = begin + j
+                rows[place, b * columns:(b + 1) * columns] = lax.dot_general(
+                    moved[j * columns:(j + 1) * columns, 0:half].T.astype(jnp.bfloat16),
+                    rotation[b], (((1,), (0,)), ((), ())),
+                    preferred_element_type=jnp.float32,
+                ).astype(jnp.bfloat16)
 
     every = (width + extra) // columns
     spans = spans_of(every)
@@ -463,11 +469,9 @@
                 elif not last:
                     total[b, at, :] += product[:, lanes]
                 else:
-                    staged[at, lanes] = (
+                    out_ref[at, lanes] = (
                         (total[b, at, :] + product[:, lanes]) * factor
                     ).astype(jnp.bfloat16)
-            if last:
-                pltpu.make_async_copy(staged.at[at, :], out_ref.at[at, :], out_sem.at[step]).start()
 
         return counted
 
@@ -491,11 +495,6 @@
     for flag, copy in sends:
         under(flag, copy.wait_send)
 
-    @pl.loop(0, width // last_tile)
-    def _(step):
-        at = pl.ds(pl.multiple_of(step * last_tile, last_tile), last_tile)
-        pltpu.make_async_copy(staged.at[at, :], out_ref.at[at, :], out_sem.at[step]).wait()
-
 
 def gathered_hessian(
     attn_partial, residual, norm_gain, channel_order, rotation, routes, slab_block
@@ -511,24 +510,21 @@
     sends = sum(op[0] == "send" for op in plan(planes, spans_of(every), groups))
     vmem = pl.BlockSpec(memory_space=pltpu.VMEM)
     smem = pl.BlockSpec(memory_space=pltpu.SMEM)
-    whole = pl.BlockSpec(memory_space=pl.ANY)
+    whole = pl.BlockSpec(memory_space=pltpu.HBM)
     return pl.pallas_call(
         functools.partial(hessian_kernel, planes, local, width, columns, extra),
-        out_shape=jax.ShapeDtypeStruct((width, SLAB), jnp.bfloat16),
+        out_shape=pltpu.VMEM((width, SLAB), jnp.bfloat16),
         in_specs=[smem, smem, whole, whole, vmem, vmem, whole],
-        out_specs=whole,
+        out_specs=vmem,
         scratch_shapes=[
             pltpu.VMEM((experts * local, width + extra), jnp.bfloat16),
             pltpu.VMEM((SLAB // columns, width, columns), jnp.float32),
-            pltpu.VMEM((width, SLAB), jnp.bfloat16),
             pltpu.VMEM((4 * local, width), jnp.bfloat16),
             pltpu.VMEM((4 * local, SLAB), jnp.bfloat16),
             pltpu.VMEM((blocks, 4 * local, columns), jnp.bfloat16),
             pltpu.VMEM(rotation.shape, jnp.bfloat16),
             pltpu.VMEM((local, width), jnp.bfloat16),
-            pltpu.VMEM((local, width), jnp.bfloat16),
-            pltpu.VMEM((local, width), jnp.bfloat16),
-            pltpu.VMEM((columns * divisor(blocks, 14), columns), jnp.float32),
+            pltpu.VMEM((columns * divisor(blocks, 7), columns), jnp.float32),
             pltpu.SemaphoreType.DMA((4,)),
             pltpu.SemaphoreType.DMA((8,)),
             pltpu.SemaphoreType.DMA((8,)),
@@ -537,10 +533,9 @@
             pltpu.SemaphoreType.DMA((sends,)),
             pltpu.SemaphoreType.DMA((experts, 3)),
             pltpu.SemaphoreType.DMA((planes, 3, 2)),
-            pltpu.SemaphoreType.DMA((width // columns // divisor(blocks, 8),)),
         ],
         compiler_params=pltpu.CompilerParams(
-            collective_id=0, has_side_effects=True, vmem_limit_bytes=67043328
+            collective_id=0, has_side_effects=True, vmem_limit_bytes=57000000
         ),
         name="gathered_hessian",
     )(channel_order, slab_block, attn_partial, residual, norm_gain[None, :], routes.T, rotation)

time: 142 us -> 138 us (0.972)
  local copies, waits for them, and re-layouts: 6.6 us -> 3.05 us
    unnamed x1, local copies, waits for them, and re-layouts: 6.6 us -> 3.05 us
where the time goes in v3:
time: 138 us
  Pallas kernels  134 us (97%)
  local copies, waits for them, and re-layouts  3.05 us (2%)
    pallas_call x1, Pallas kernels, gathered_hessian(): pl.pallas_call(functools.partial(hessian_kernel, planes, local, width, co...  134 us
    unnamed x1, local copies, waits for them, and re-layouts  3.05 us

profile of v3, /device:TPU:0, one launch (start us, length us, event | category | flops | bytes accessed | tf_op | source)
XLA Modules:
  0.0 137.7 jit_solution(11244699148498284132)
XLA Ops:
  0.7 134.0 %gathered_hessian.1 = bf16[7168,512]{1,0:T(8,128)(2,1)S(1)} custom-call(s32[7168]{0:T(1024)} %order_ref.1, s32[1]{0:T(128)S(6)} %copy.10.block_ref, bf16[1,256,7168]{2,1,0:T(8,128)(2,1)} %partial_ref.1, bf16[64,7168]{1,0:T(8,128)(2,1)} %residual_ref.1, f32[1,7168]{1,0:T(1,128)} %bitcast.4, s32[8,64]{1,0:T(8,128)} %bitcast.5, bf16[56,128,128]{2,1,0:T(8,128)(2,1)} %rotation_ref.1), custom_call_target="tpu_custom_call" | custom-call | tf_op jit(solution)/shard_map/gathered_hessian/pallas_call | solution.py:514
  134.6 3.1 %copy.9 = bf16[1,7168,512]{2,1,0:T(8,128)(2,1)} copy(bf16[1,7168,512]{2,1,0:T(8,128)(2,1)S(1)} %bitcast.3) | data formatting | bytes 14680064
